TPU v7x, 768 devices: a whole 4x8x12 slice. The times are simulated.
768 devices in a mesh: orb: 64 (over y, z_hi, core), dom: 12 (over z_lo, x).
Axes of the slice: x: 4, y: 8, z: 12 (z_hi: 4, z_lo: 3; z = z_hi * 3 + z_lo), core: 2. Of those that a mesh axis runs over, the one named last changes fastest.
Arguments:
- psi: float32 [2, 64, 96, 16, 128], P(None, 'orb', 'dom'), may hold values from -6 to 6
- occupations: float32 [64], P('orb'), may hold values from 0.5 to 2
- core_density: float32 [96, 16, 128], P('dom'), may hold values from 0.1 to 0.5
- external: float32 [96, 16, 128], P('dom'), may hold values from -3 to 3
Outputs:
- psi_next: float32 [2, 64, 96, 16, 128], P(None, 'orb', 'dom')
- v_mid: float32 [96, 16, 128], P('dom')
All inputs are finite; a program needn't handle non-finite values.
Results may differ from a plain program's by a relative error of at most 0.00021.
Values sent between devices are 32-bit elements; how exact they have to be, the bound alone decides.
A program may use at most 32 MiB of HBM per device.

v0:
```python
import math

import jax
import jax.numpy as jnp
from jax import lax
from jax.sharding import PartitionSpec as P

coeff_zero = -2.5
coeff_one = 4.0 / 3.0
coeff_two = -1.0 / 12.0
time_step = 0.5
exch_coeff = -((3.0 / math.pi) ** (1.0 / 3.0))


def padded(value, sides, width):
    for axis, dim in sides:
        size, length = (lax.axis_size(axis), value.shape[dim])
        up = [(i, (i + 1) % size) for i in range(size)]
        down = [(j, i) for i, j in up]
        last = lax.slice_in_dim(value, length - width, length, axis=dim)
        leading = lax.slice_in_dim(value, 0, width, axis=dim)
        before = lax.ppermute(last, axis, up)
        after = lax.ppermute(leading, axis, down)
        value = jnp.concatenate([before, value, after], axis=dim)
    return value


def cut_along(value, dim, size):
    lengths = value.shape
    pieces = value.reshape(*lengths[:dim], size, lengths[dim] // size, *lengths[dim + 1 :])
    return jnp.moveaxis(pieces, dim, 0)


def summed_on_arrival(value, axis, dim):
    size = lax.axis_size(axis)
    pieces = lax.all_to_all(cut_along(value, dim, size), axis, 0, 0, tiled=True)
    return jnp.sum(pieces, axis=0)


def copy_for_each(value, axis):
    size = lax.axis_size(axis)
    return lax.all_to_all(
        jnp.broadcast_to(value[None], (size, *value.shape)), axis, 0, 0, tiled=True
    )


def in_order(pieces, dim):
    pieces = jnp.moveaxis(pieces, 0, dim)
    lengths = pieces.shape
    return pieces.reshape(*lengths[:dim], lengths[dim] * lengths[dim + 1], *lengths[dim + 2 :])


def collect(value, axis, dim):
    pieces = copy_for_each(value, axis)
    return in_order(pieces, dim)


def second_local(field, axis):
    near = jnp.roll(field, 1, axis) + jnp.roll(field, -1, axis)
    far = jnp.roll(field, 2, axis) + jnp.roll(field, -2, axis)
    return coeff_zero * field + coeff_one * near + coeff_two * far


def lap_trim(field):
    width = field.shape[2] - 4
    middle = field[:, :, 2 : width + 2]
    near = field[:, :, 1 : width + 1] + field[:, :, 3 : width + 3]
    far = field[:, :, 0:width] + field[:, :, 4 : width + 4]
    along_x = coeff_zero * middle + coeff_one * near + coeff_two * far
    return along_x + second_local(middle, 3) + second_local(middle, 4)


def next_term(image, order):
    return jnp.stack([time_step * image[1] / order, -time_step * image[0] / order])


def taylor_deep(potential, padded_psi, lap_first):
    cells = potential.shape[0]
    widened = padded(potential, (("dom", 0),), 6)

    def centre(field):
        offset = (field.shape[2] - cells) // 2
        return field[:, :, offset : offset + cells]

    total = centre(padded_psi)
    term = padded_psi
    lap = lap_first
    for order in range(1, 5):
        width = lap.shape[2]
        offset = (widened.shape[0] - width) // 2
        local_pot = widened[offset : offset + width]
        image = -0.5 * lap + local_pot[None, None] * term[:, :, 2 : width + 2]
        term = next_term(image, order)
        total = total + centre(term)
        if order < 4:
            lap = lap_trim(term)
    return total


def partial_density(orbitals, occupations):
    squares = orbitals[0] * orbitals[0] + orbitals[1] * orbitals[1]
    return jnp.tensordot(occupations, squares, axes=1, precision=lax.Precision.HIGHEST)


def share_sum(partial_value):
    return summed_on_arrival(partial_value.reshape(-1), "orb", 0)


def spread(share, shape):
    return collect(share, "orb", 0).reshape(shape)


def shards(psi, occupations, core_density, external):
    total_orbs = occupations.shape[0] * lax.axis_size("orb")
    shape = core_density.shape
    padded_psi = padded(psi, (("dom", 2),), 8)
    lap_first = lap_trim(padded_psi)

    def propagate(potential):
        return taylor_deep(potential, padded_psi, lap_first)

    count = core_density.size // lax.axis_size("orb")
    start = lax.axis_index("orb") * count
    core_share = lax.dynamic_slice_in_dim(core_density.reshape(-1), start, count)
    ext_share = lax.dynamic_slice_in_dim(external.reshape(-1), start, count)
    vx_start = exch_coeff * jnp.cbrt(
        core_share + share_sum(partial_density(psi, occupations)) / total_orbs
    )
    v_start = spread(ext_share + vx_start, shape)
    psi_pred = propagate(v_start)
    vx_pred = exch_coeff * jnp.cbrt(
        core_share + share_sum(partial_density(psi_pred, occupations)) / total_orbs
    )
    v_mid = spread(ext_share + 0.5 * (vx_start + vx_pred), shape)
    psi_next = propagate(v_mid)
    return (psi_next, v_mid)


def solution(mesh):
    in_specs = (
        P(None, "orb", "dom", None, None),
        P("orb"),
        P("dom", None, None),
        P("dom", None, None),
    )
    out_specs = (P(None, "orb", "dom", None, None), P("dom", None, None))
    return jax.shard_map(shards, mesh=mesh, in_specs=in_specs, out_specs=out_specs, check_vma=False)
```

profile of v0, /device:TPU:1, one launch (start us, length us, event | category | flops | bytes accessed | tf_op | source)
XLA Modules:
  0.0 141.7 jit_solution(15215896204350638877)
XLA Ops:
  0.6 4.0 %collective-permute-start = (f32[2,1,8,16,128]{4,3,2,1,0:T(8,128)}, f32[2,1,8,16,128]{4,3,2,1,0:T(8,128)S(1)}, u32[]{:S(2)}, u32[]{:S(2)}) collective-permute-start(f32[2,1,8,16,128]{4,3,2,1,0:T(8,128)} %param.4), channel_id=1, source_target_pairs={{0,1},{1,2},{2,3},{3,4},{4,5},{5,6},{6,7},{7,8},{8,9},{9,10},{10,1... | collective-permute-start | bytes 393224 | tf_op jit(solution)/shard_map/ppermute | solution.py:22
  4.6 6.8 %collective-permute-start.1 = (f32[2,1,8,16,128]{4,3,2,1,0:T(8,128)}, f32[2,1,8,16,128]{4,3,2,1,0:T(8,128)S(1)}, u32[]{:S(2)}, u32[]{:S(2)}) collective-permute-start(f32[2,1,8,16,128]{4,3,2,1,0:T(8,128)} %param.4), channel_id=1, source_target_pairs={{1,0},{2,1},{3,2},{4,3},{5,4},{6,5},{7,6},{8,7},{9,8},{10,9},{11,1... | collective-permute-start | bytes 393224 | tf_op jit(solution)/shard_map/ppermute | solution.py:23
  12.0 1.5 %add_multiply_fusion = f32[1,1,8,16,128]{4,3,2,1,0:T(8,128)} fusion(f32[2,1,8,16,128]{4,3,2,1,0:T(8,128)} %param.4, f32[]{:T(128)} %bitcast.11), kind=kLoop, calls=%fused_computation.545 | loop fusion | flops 65536 | bytes 196612 | tf_op jit(solution)/shard_map/dot_general | solution.py:102
  13.6 21.1 %all-to-all-start = ((f32[64,1,256]{2,1,0:T(1,128)}), f32[64,1,256]{2,1,0:T(1,128)S(1)}, u32[]{:S(2)}, u32[]{:S(2)}) async-start(f32[64,1,256]{2,1,0:T(1,128)} %bitcast.3), calls=%async_computation | async-start | bytes 131072 | tf_op jit(solution)/shard_map/all_to_all | solution.py:36
  34.8 0.9 copy-done
  35.7 0.2 fusion.274
  35.9 0.2 fusion.275
  36.0 0.2 fusion.276
  36.2 0.9 fusion.277
  37.1 0.9 fusion.271
  38.0 11.2 %all-to-all-done = f32[64,1,256]{2,1,0:T(1,128)S(1)} async-done(((f32[64,1,256]{2,1,0:T(1,128)}), f32[64,1,256]{2,1,0:T(1,128)S(1)}, u32[]{:S(2)}, u32[]{:S(2)}) %all-to-all-start) | async-done | bytes 65568 | tf_op jit(solution)/shard_map/all_to_all | solution.py:36
  49.3 0.8 dynamic-slice_add_fusion
  50.1 0.7 broadcast_in_dim.4
  50.8 4.4 %all-to-all-start.1 = ((f32[64,1,256]{2,1,0:T(1,128)}), f32[64,1,256]{2,1,0:T(1,128)S(1)}, u32[]{:S(2)}, u32[]{:S(2)}) async-start(f32[64,1,256]{2,1,0:T(1,128)} %broadcast_in_dim.4), calls=%async_computation.1 | async-start | bytes 131072 | tf_op jit(solution)/shard_map/all_to_all | solution.py:42
  55.2 0.7 fusion.272
  55.9 14.0 %all-to-all-done.1 = f32[64,1,256]{2,1,0:T(1,128)S(1)} async-done(((f32[64,1,256]{2,1,0:T(1,128)}), f32[64,1,256]{2,1,0:T(1,128)S(1)}, u32[]{:S(2)}, u32[]{:S(2)}) %all-to-all-start.1) | async-done | bytes 65568 | tf_op jit(solution)/shard_map/all_to_all | solution.py:42
  69.9 2.1 %collective-permute-start.2 = (f32[6,16,128]{2,1,0:T(8,128)S(1)}, f32[6,16,128]{2,1,0:T(8,128)S(1)}, u32[]{:S(2)}, u32[]{:S(2)}) collective-permute-start(f32[6,16,128]{2,1,0:T(8,128)S(1)} %bitcast.20), channel_id=1, source_target_pairs={{0,1},{1,2},{2,3},{3,4},{4,5},{5,6},{6,7},{7,8},{8,9},{9,10},{10,1... | collective-permute-start | bytes 147464 | tf_op jit(solution)/shard_map/ppermute | solution.py:22
  71.9 6.4 %collective-permute-start.3 = (f32[6,16,128]{2,1,0:T(8,128)S(1)}, f32[6,16,128]{2,1,0:T(8,128)S(1)}, u32[]{:S(2)}, u32[]{:S(2)}) collective-permute-start(f32[6,16,128]{2,1,0:T(8,128)S(1)} %bitcast.19), channel_id=1, source_target_pairs={{1,0},{2,1},{3,2},{4,3},{5,4},{6,5},{7,6},{8,7},{9,8},{10,9},{11,1... | collective-permute-start | bytes 147464 | tf_op jit(solution)/shard_map/ppermute | solution.py:23
  78.4 1.1 collective-permute-done.3
  79.5 0.7 copy-done.3
  80.3 2.4 %multiply_add_fusion.1 = (f32[2,1,20,16,128]{4,3,2,1,0:T(8,128)S(1)}, f32[2,1,20,16,128]{4,3,2,1,0:T(8,128)}) fusion(f32[2,1,24,16,128]{4,3,2,1,0:T(8,128)S(1)} %constant_dynamic-update-slice_fusion, f32[20,16,128]{2,1,0:T(8,128)S(1)} %pad_maximum_fusion.4, f32[2,1,20,16,2]{4,3,2,1,0:T(8,128)S(1)} %get-tuple-element.17, ...), kind=kLoop, calls=%fused_computation.270 | loop fusion | flops 2621440 | bytes 5079040 | tf_op jit(solution)/shard_map/add | solution.py:92
  82.8 0.1 fusion.65
  82.9 0.1 fusion.41
  83.0 0.1 fusion.64
  83.2 0.1 fusion.63
  83.5 0.5 fusion.51
  84.3 0.1 fusion.136
  84.4 0.1 fusion.135
  84.7 0.4 fusion.123
  85.6 0.3 fusion.195
  86.0 20.8 %all_to_all.30 = f32[64,1,256]{2,1,0:T(1,128)S(1)} all-to-all(f32[64,1,256]{2,1,0:T(1,128)S(1)} %bitcast.18), channel_id=1, replica_groups=mesh['orb'=64,'dom'=12] {'orb'}, dimensions={0} | all-to-all | bytes 131072 | tf_op jit(solution)/shard_map/all_to_all | solution.py:36
  106.9 0.8 multiply_add_fusion.2
  107.8 18.5 %all_to_all.31 = f32[64,1,256]{2,1,0:T(1,128)S(1)} all-to-all(f32[64,1,256]{2,1,0:T(1,128)S(1)} %broadcast_in_dim.5), channel_id=1, replica_groups=mesh['orb'=64,'dom'=12] {'orb'}, dimensions={0} | all-to-all | bytes 131072 | tf_op jit(solution)/shard_map/all_to_all | solution.py:42
  126.3 1.9 %collective-permute-start.4 = (f32[6,16,128]{2,1,0:T(8,128)S(1)}, f32[6,16,128]{2,1,0:T(8,128)S(1)}, u32[]{:S(2)}, u32[]{:S(2)}) collective-permute-start(f32[6,16,128]{2,1,0:T(8,128)S(1)} %bitcast.22), channel_id=1, source_target_pairs={{0,1},{1,2},{2,3},{3,4},{4,5},{5,6},{6,7},{7,8},{8,9},{9,10},{10,1... | collective-permute-start | bytes 147464 | tf_op jit(solution)/shard_map/ppermute | solution.py:22
  128.2 7.7 %collective-permute-start.5 = (f32[6,16,128]{2,1,0:T(8,128)S(1)}, f32[6,16,128]{2,1,0:T(8,128)S(1)}, u32[]{:S(2)}, u32[]{:S(2)}) collective-permute-start(f32[6,16,128]{2,1,0:T(8,128)S(1)} %bitcast.21), channel_id=1, source_target_pairs={{1,0},{2,1},{3,2},{4,3},{5,4},{6,5},{7,6},{8,7},{9,8},{10,9},{11,1... | collective-permute-start | bytes 147464 | tf_op jit(solution)/shard_map/ppermute | solution.py:23
  135.9 1.1 collective-permute-done.5
  137.2 0.1 fusion.39
  137.3 0.1 fusion.15
  137.5 0.1 fusion.38
  137.6 0.1 fusion.37
  137.9 0.5 fusion.25
  138.6 0.1 fusion.87
  138.7 0.1 fusion.110
  138.8 0.1 fusion.109
  139.1 0.4 fusion.97
  140.0 0.3 fusion.169
  140.3 0.7 fusion.214
  141.0 0.6 copy.10
  (74 shorter events, 2.5 us)
Async XLA Ops:
  0.6 34.1 %collective-permute-start = (f32[2,1,8,16,128]{4,3,2,1,0:T(8,128)}, f32[2,1,8,16,128]{4,3,2,1,0:T(8,128)S(1)}, u32[]{:S(2)}, u32[]{:S(2)}) collective-permute-start(f32[2,1,8,16,128]{4,3,2,1,0:T(8,128)} %param.4), channel_id=1, source_target_pairs={{0,1},{1,2},{2,3},{3,4},{4,5},{5,6},{6,7},{7,8},{8,9},{9,10},{10,1... | collective-permute-start | bytes 393224 | tf_op jit(solution)/shard_map/ppermute | solution.py:22
  4.6 31.0 %collective-permute-start.1 = (f32[2,1,8,16,128]{4,3,2,1,0:T(8,128)}, f32[2,1,8,16,128]{4,3,2,1,0:T(8,128)S(1)}, u32[]{:S(2)}, u32[]{:S(2)}) collective-permute-start(f32[2,1,8,16,128]{4,3,2,1,0:T(8,128)} %param.4), channel_id=1, source_target_pairs={{1,0},{2,1},{3,2},{4,3},{5,4},{6,5},{7,6},{8,7},{9,8},{10,9},{11,1... | collective-permute-start | bytes 393224 | tf_op jit(solution)/shard_map/ppermute | solution.py:23
  13.6 35.6 %all-to-all-start = ((f32[64,1,256]{2,1,0:T(1,128)}), f32[64,1,256]{2,1,0:T(1,128)S(1)}, u32[]{:S(2)}, u32[]{:S(2)}) async-start(f32[64,1,256]{2,1,0:T(1,128)} %bitcast.3), calls=%async_computation | async-start | bytes 131072 | tf_op jit(solution)/shard_map/all_to_all | solution.py:36
  34.7 0.9 copy-start
  50.8 19.1 %all-to-all-start.1 = ((f32[64,1,256]{2,1,0:T(1,128)}), f32[64,1,256]{2,1,0:T(1,128)S(1)}, u32[]{:S(2)}, u32[]{:S(2)}) async-start(f32[64,1,256]{2,1,0:T(1,128)} %broadcast_in_dim.4), calls=%async_computation.1 | async-start | bytes 131072 | tf_op jit(solution)/shard_map/all_to_all | solution.py:42
  69.8 9.7 %copy-start.1 = (f32[2,1,20,16,126]{4,3,2,1,0:T(8,128)S(1)}, f32[2,1,20,16,126]{4,3,2,1,0:T(8,128)}, u32[]{:S(2)}) copy-start(f32[2,1,20,16,126]{4,3,2,1,0:T(8,128)} %get-tuple-element.19) | copy-start | bytes 967684
  69.9 8.5 %collective-permute-start.2 = (f32[6,16,128]{2,1,0:T(8,128)S(1)}, f32[6,16,128]{2,1,0:T(8,128)S(1)}, u32[]{:S(2)}, u32[]{:S(2)}) collective-permute-start(f32[6,16,128]{2,1,0:T(8,128)S(1)} %bitcast.20), channel_id=1, source_target_pairs={{0,1},{1,2},{2,3},{3,4},{4,5},{5,6},{6,7},{7,8},{8,9},{9,10},{10,1... | collective-permute-start | bytes 147464 | tf_op jit(solution)/shard_map/ppermute | solution.py:22
  71.9 7.5 %collective-permute-start.3 = (f32[6,16,128]{2,1,0:T(8,128)S(1)}, f32[6,16,128]{2,1,0:T(8,128)S(1)}, u32[]{:S(2)}, u32[]{:S(2)}) collective-permute-start(f32[6,16,128]{2,1,0:T(8,128)S(1)} %bitcast.19), channel_id=1, source_target_pairs={{1,0},{2,1},{3,2},{4,3},{5,4},{6,5},{7,6},{8,7},{9,8},{10,9},{11,1... | collective-permute-start | bytes 147464 | tf_op jit(solution)/shard_map/ppermute | solution.py:23
  79.5 0.8 copy-start.3
  79.5 0.8 copy-start.4
  107.8 29.3 %copy-start.2 = (f32[2,1,20,16,128]{4,3,2,1,0:T(8,128)S(1)}, f32[2,1,20,16,128]{4,3,2,1,0:T(8,128)}, u32[]{:S(2)}) copy-start(f32[2,1,20,16,128]{4,3,2,1,0:T(8,128)} %get-tuple-element.3) | copy-start | bytes 983044
  126.3 9.6 %collective-permute-start.4 = (f32[6,16,128]{2,1,0:T(8,128)S(1)}, f32[6,16,128]{2,1,0:T(8,128)S(1)}, u32[]{:S(2)}, u32[]{:S(2)}) collective-permute-start(f32[6,16,128]{2,1,0:T(8,128)S(1)} %bitcast.22), channel_id=1, source_target_pairs={{0,1},{1,2},{2,3},{3,4},{4,5},{5,6},{6,7},{7,8},{8,9},{9,10},{10,1... | collective-permute-start | bytes 147464 | tf_op jit(solution)/shard_map/ppermute | solution.py:22
  128.2 8.9 %collective-permute-start.5 = (f32[6,16,128]{2,1,0:T(8,128)S(1)}, f32[6,16,128]{2,1,0:T(8,128)S(1)}, u32[]{:S(2)}, u32[]{:S(2)}) collective-permute-start(f32[6,16,128]{2,1,0:T(8,128)S(1)} %bitcast.21), channel_id=1, source_target_pairs={{1,0},{2,1},{3,2},{4,3},{5,4},{6,5},{7,6},{8,7},{9,8},{10,9},{11,1... | collective-permute-start | bytes 147464 | tf_op jit(solution)/shard_map/ppermute | solution.py:23
where the time goes:
time: 142 us
  starting transfers between devices  54.4 us (38%)
  blocking collectives  39.3 us (28%)
  waiting for transfers between devices  27.4 us (19%)
  other arithmetic  12.5 us (9%)
  local copies, waits for them, and re-layouts  6.17 us (4%)
  between operations  1.96 us (1%)
    all_to_all x1, starting transfers between devices, summed_on_arrival(): pieces = lax.all_to_all(cut_along(value, dim, size), axis, 0, 0, tiled=True)  21.1 us
    ppermute x3, starting transfers between devices, padded(): after = lax.ppermute(leading, axis, down)  20.9 us
    all_to_all x1, blocking collectives, summed_on_arrival(): pieces = lax.all_to_all(cut_along(value, dim, size), axis, 0, 0, tiled=True)  20.8 us
    all_to_all x1, blocking collectives, copy_for_each(): lax.all_to_all(jnp.broadcast_to(value[None], (size, *value.shape)), axis,...  18.5 us
    all_to_all x1, waiting for transfers between devices, copy_for_each(): lax.all_to_all(jnp.broadcast_to(value[None], (size, *value.shape)), axis,...  14 us
    all_to_all x1, waiting for transfers between devices, summed_on_arrival(): pieces = lax.all_to_all(cut_along(value, dim, size), axis, 0, 0, tiled=True)  11.2 us
    ppermute x3, starting transfers between devices, padded(): before = lax.ppermute(last, axis, up)  7.92 us
    add x8, other arithmetic, taylor_deep(): image = -0.5 * lap + local_pot[None, None] * term[:, :, 2:width + 2]  4.91 us
  transfers between devices with their start and end apart: 8, of which 4 were waited for; matrix products, arithmetic and copies ran while one was open for 3% of the time, Pallas kernels for 0%

commit v1 on v0

v1 whole, which is shorter than its diff:
```python
import math

import jax
import jax.numpy as jnp
from jax import lax
from jax.experimental import pallas as pl
from jax.experimental.pallas import tpu as pltpu
from jax.sharding import PartitionSpec as P

time_step = 0.5
exch_coeff = -((3.0 / math.pi) ** (1.0 / 3.0))
MESH = pl.DeviceIdType.MESH

NYR, NZR, NCORE, NDOM, ORBS = 8, 4, 2, 12, 64
LAYERS, ROWS, HALF, LANES = 8, 16, 8, 128

Y_FAR = (4, 3, 5, 2, 6, 1, 7)
Y_NEAR = Y_FAR[::-1]
Z_OFFS = tuple((dd, dz) for dz in (2, 1, 3, 0) for dd in (-1, 1, 0) if (dd, dz) != (0, 0))
CHUNKS = {
    1: ((2, 2), (4, 4), (8, 4), (12, 4), (16, 4), (20, 2)),
    2: ((4, 4), (8, 4), (12, 4), (16, 4)),
    3: ((6, 2), (8, 4), (12, 4), (16, 2)),
    4: ((8, 4), (12, 4)),
}


def code(dd):
    return (0, 1, 2)[dd]


def z_slot(dd, dz):
    return code(dd) * NZR + dz


def stencil(ref, comp, first, count):
    field = ref[comp, first - 2 : first + count + 2]
    mid = field[2 : count + 2]
    near = field[1 : count + 1] + field[3 : count + 3]
    far = field[0:count] + field[4 : count + 4]
    near = near + (pltpu.roll(mid, 1, 1) + pltpu.roll(mid, ROWS - 1, 1))
    far = far + (pltpu.roll(mid, 2, 1) + pltpu.roll(mid, ROWS - 2, 1))
    near = near + (pltpu.roll(mid, 1, 2) + pltpu.roll(mid, LANES - 1, 2))
    far = far + (pltpu.roll(mid, 2, 2) + pltpu.roll(mid, LANES - 2, 2))
    return mid, near, far


def exchange_term(density):
    return exch_coeff * jnp.exp(jnp.log(density) * (1.0 / 3.0))


def kernel(
    occ_ref, psi_hbm, core_hbm, ext_hbm, psi_out, vmid_out,
    padded, lap1, t1, t2, t3, result, slabs, vx0, dens, dens_in, pair, y_in, z_in, vslab, pot,
    load_sem, halo_s, halo_r, slab_s, slab_r, pair_s, pair_r, y_s, y_r, z_s, z_r, g_s, g_r, f_s, f_r, out_sem,
):
    d = lax.axis_index("dom")
    o = lax.axis_index("orb")
    y = lax.div(o, NZR * NCORE)
    z = lax.rem(lax.div(o, NCORE), NZR)
    c = lax.rem(o, NCORE)
    other = 1 - c

    def peer(dd=0, dy=0, dz=0, dc=0):
        y2 = lax.rem(y + dy, NYR)
        z2 = lax.rem(z + dz, NZR)
        c2 = other if dc else c
        return {"dom": lax.rem(d + dd + NDOM, NDOM), "orb": (y2 * NZR + z2) * NCORE + c2}

    def remote(src, dst, send, recv, target):
        return pltpu.make_async_remote_copy(
            src_ref=src, dst_ref=dst, send_sem=send, recv_sem=recv, device_id=target, device_id_type=MESH
        )

    mine = pl.ds(pl.multiple_of(c * HALF, HALF), HALF)
    theirs = pl.ds(pl.multiple_of(other * HALF, HALF), HALF)
    centre = pl.ds(LAYERS, LAYERS)

    load_psi = pltpu.make_async_copy(psi_hbm, padded.at[:, centre], load_sem.at[0])
    load_core = pltpu.make_async_copy(core_hbm.at[y, mine], slabs.at[0, 0], load_sem.at[1])
    load_ext = pltpu.make_async_copy(ext_hbm.at[y, mine], slabs.at[0, 1], load_sem.at[2])
    load_psi.start()
    load_core.start()
    load_ext.start()

    barrier = pltpu.get_barrier_semaphore()
    partners = [peer(dc=1)] + [peer(dy=k) for k in Y_FAR] + [peer(dd=a, dz=b) for a, b in Z_OFFS]
    for target in partners:
        pl.semaphore_signal(barrier, inc=1, device_id=target, device_id_type=MESH)

    occ = occ_ref[0]
    waits = []

    def put_density(r, first, count, re, im):
        value = occ * (re * re + im * im)
        dens[r, 0, first : first + count] = value[:, :HALF]
        dens[r, 1, first : first + count] = value[:, HALF:]

    def reduce_to_slab(r, after_y_sent):
        swap = remote(dens.at[r, other], dens_in.at[r], pair_s.at[r], pair_r.at[r], peer(dc=1))
        swap.start()
        swap.wait_recv()
        waits.append(swap)
        pair[r] = dens[r, c] + dens_in[r]
        copies = {}
        for k in Y_FAR:
            y2 = lax.rem(y + k, NYR)
            copies[k] = remote(
                pair.at[r, y2], y_in.at[r, k - 1], y_s.at[r, k - 1], y_r.at[r, k - 1], peer(dy=k)
            )
            copies[k].start()
        after_y_sent()
        total = pair[r, y]
        for k in Y_NEAR:
            copies[k].wait_recv()
            total = total + y_in[r, k - 1]
        waits.extend(copies.values())
        z_in[r, 0] = total
        copies = {}
        for dd, dz in Z_OFFS:
            slot = z_slot(dd, dz)
            copies[dd, dz] = remote(
                z_in.at[r, 0], z_in.at[r, slot], z_s.at[r, slot], z_r.at[r, slot], peer(dd=dd, dz=dz)
            )
            copies[dd, dz].start()
        return copies

    def finish_slab(r, copies):
        for key in reversed(Z_OFFS):
            copies[key].wait_recv()
        waits.extend(copies.values())
        found = []
        for dd in (1, 0, -1):
            base = code(dd) * NZR
            summed = (z_in[r, base] + z_in[r, base + 2]) + (z_in[r, base + 1] + z_in[r, base + 3])
            found.append(exchange_term(slabs[code(dd), 0] + summed * (1.0 / ORBS)))
        return found

    def gather(r, while_waiting):
        pot[r, :, y, mine] = vslab[r]
        copies = {}
        for k in Y_FAR:
            copies[k] = remote(
                vslab.at[r], pot.at[r, :, y, mine], g_s.at[r, k - 1], g_r.at[r, k - 1], peer(dy=k)
            )
            copies[k].start()
        forwards = []

        def forward(k):
            layer = lax.rem(y + NYR - k, NYR)
            copy = remote(
                pot.at[r, :, layer, mine], pot.at[r, :, layer, mine], f_s.at[r, k], f_r.at[r, k], peer(dc=1)
            )
            copy.start()
            forwards.append(copy)

        forward(0)
        while_waiting()
        for k in Y_NEAR:
            copies[k].wait_recv()
            forward(k)
        for copy in forwards:
            copy.wait_recv()
        waits.extend(copies.values())
        waits.extend(forwards)

    def local_pot(r, first, count):
        block, offset = divmod(first, LAYERS)
        return pot[r, block, offset : offset + count]

    def first_order():
        for comp in range(2):
            for first, count in CHUNKS[1]:
                mid, near, far = stencil(padded, comp, first, count)
                lap1[comp, first : first + count] = 3.75 * mid - (2.0 / 3.0) * near + (1.0 / 24.0) * far

    def propagate(r, emit):
        for first, count in CHUNKS[1]:
            there = slice(first, first + count)
            v = local_pot(r, first, count)
            step = time_step
            t1[0, there] = step * (lap1[1, there] + v * padded[1, there])
            t1[1, there] = -step * (lap1[0, there] + v * padded[0, there])
        for order, src, dst in ((2, t1, t2), (3, t2, t3)):
            step = time_step / order
            for first, count in CHUNKS[order]:
                there = slice(first, first + count)
                v = step * local_pot(r, first, count) + step * 3.75
                mid, near, far = stencil(src, 1, first, count)
                dst[0, there] = v * mid - (step * 2.0 / 3.0) * near + (step / 24.0) * far
                mid, near, far = stencil(src, 0, first, count)
                dst[1, there] = (step * 2.0 / 3.0) * near - v * mid - (step / 24.0) * far
        step = time_step / 4
        for first, count in CHUNKS[4]:
            there = slice(first, first + count)
            v = step * local_pot(r, first, count) + step * 3.75
            mid, near, far = stencil(t3, 1, first, count)
            re = v * mid - (step * 2.0 / 3.0) * near + (step / 24.0) * far
            re = re + ((padded[0, there] + t1[0, there]) + (t2[0, there] + t3[0, there]))
            mid, near, far = stencil(t3, 0, first, count)
            im = (step * 2.0 / 3.0) * near - v * mid - (step / 24.0) * far
            im = im + ((padded[1, there] + t1[1, there]) + (t2[1, there] + t3[1, there]))
            emit(first - LAYERS, count, re, im)

    load_psi.wait()
    for first in (0, 4):
        there = pl.ds(LAYERS + first, 4)
        put_density(0, first, 4, padded[0, there], padded[1, there])
    load_core.wait()
    load_ext.wait()
    pl.semaphore_wait(barrier, len(partners))

    halo = {
        1: remote(padded.at[:, centre], padded.at[:, pl.ds(0, LAYERS)], halo_s.at[0], halo_r.at[0], peer(dd=1)),
        -1: remote(
            padded.at[:, centre], padded.at[:, pl.ds(2 * LAYERS, LAYERS)], halo_s.at[1], halo_r.at[1], peer(dd=-1)
        ),
    }
    slab_copies = [
        remote(slabs.at[0], slabs.at[code(dd)], slab_s.at[code(dd)], slab_r.at[code(dd)], peer(dd=dd))
        for dd in (1, -1)
    ]

    def send_halo():
        for copy in slab_copies:
            copy.start()
        for copy in halo.values():
            copy.start()

    def nothing():
        pass

    sent = reduce_to_slab(0, send_halo)
    for copy in slab_copies:
        copy.wait_recv()
    waits.extend(slab_copies)
    for index, value in enumerate(finish_slab(0, sent)):
        slot = (1, 0, 2)[index]
        vx0[index] = value
        vslab[0, index] = slabs[slot, 1] + value

    def wait_halo():
        for copy in halo.values():
            copy.wait_recv()
        waits.extend(halo.values())
        first_order()

    gather(0, wait_halo)
    propagate(0, lambda first, count, re, im: put_density(1, first, count, re, im))

    sent = reduce_to_slab(1, nothing)
    for index, value in enumerate(finish_slab(1, sent)):
        slot = (1, 0, 2)[index]
        vslab[1, index] = slabs[slot, 1] + 0.5 * (vx0[index] + value)
    gather(1, nothing)

    store_pot = pltpu.make_async_copy(pot.at[1, 1], vmid_out, out_sem.at[0])
    store_pot.start()
    stores = [store_pot]

    def emit_result(first, count, re, im):
        there = slice(first, first + count)
        result[0, there] = re
        result[1, there] = im
        copy = pltpu.make_async_copy(
            result.at[:, pl.ds(first, count)], psi_out.at[:, pl.ds(first, count)], out_sem.at[1 + first // 4]
        )
        copy.start()
        stores.append(copy)

    propagate(1, emit_result)
    for copy in waits:
        copy.wait_send()
    for copy in stores:
        copy.wait()


def shards(psi, occupations, core_density, external):
    f32 = jnp.float32
    dma = pltpu.SemaphoreType.DMA
    brick = (2, LAYERS, ROWS, LANES)
    wide = (2, 3 * LAYERS, ROWS, LANES)
    tile = (HALF, LANES)
    anywhere = pl.BlockSpec(memory_space=pl.ANY)
    psi_next, v_mid = pl.pallas_call(
        kernel,
        out_shape=(jax.ShapeDtypeStruct(brick, f32), jax.ShapeDtypeStruct(core_density.shape, f32)),
        in_specs=[pl.BlockSpec(memory_space=pltpu.SMEM), anywhere, anywhere, anywhere],
        out_specs=(anywhere, anywhere),
        scratch_shapes=[
            pltpu.VMEM(wide, f32),
            pltpu.VMEM(wide, f32),
            pltpu.VMEM(wide, f32),
            pltpu.VMEM(wide, f32),
            pltpu.VMEM(wide, f32),
            pltpu.VMEM(brick, f32),
            pltpu.VMEM((3, 2, *tile), f32),
            pltpu.VMEM((3, *tile), f32),
            pltpu.VMEM((2, 2, LAYERS, *tile), f32),
            pltpu.VMEM((2, LAYERS, *tile), f32),
            pltpu.VMEM((2, LAYERS, *tile), f32),
            pltpu.VMEM((2, 7, *tile), f32),
            pltpu.VMEM((2, 12, *tile), f32),
            pltpu.VMEM((2, 3, *tile), f32),
            pltpu.VMEM((2, 3, LAYERS, ROWS, LANES), f32),
            dma((3,)), dma((2,)), dma((2,)), dma((3,)), dma((3,)), dma((2,)), dma((2,)), dma((2, 7)), dma((2, 7)),
            dma((2, 12)), dma((2, 12)), dma((2, 7)), dma((2, 7)), dma((2, 8)), dma((2, 8)), dma((3,)),
        ],
        compiler_params=pltpu.CompilerParams(collective_id=0, has_side_effects=True),
    )(occupations, psi.reshape(brick), core_density, external)
    return psi_next.reshape(psi.shape), v_mid


def solution(mesh):
    in_specs = (
        P(None, "orb", "dom", None, None),
        P("orb"),
        P("dom", None, None),
        P("dom", None, None),
    )
    out_specs = (P(None, "orb", "dom", None, None), P("dom", None, None))
    return jax.shard_map(shards, mesh=mesh, in_specs=in_specs, out_specs=out_specs, check_vma=False)
```

time: 142 us -> 61.8 us (0.44)
  Pallas kernels: 0 us -> 58.1 us
  starting transfers between devices: 54.4 us -> 0 us
  blocking collectives: 39.3 us -> 0 us
  waiting for transfers between devices: 27.4 us -> 0 us
  other arithmetic: 12.5 us -> 0 us
  local copies, waits for them, and re-layouts: 6.17 us -> 2.23 us
    pallas_call x0 -> x1, Pallas kernels: none -> 58.1 us  [shards(): pl.pallas_call(kernel, out_shape=(jax.ShapeDtypeStruct(brick, f32), jax.S...]
    all_to_all x2 -> x0, blocking collectives: 39.3 us -> none  [the longest x1 20.8 us: summed_on_arrival(): pieces = lax.all_to_all(cut_along(value, dim, size), axis, 0, 0, tiled=True)]
    ppermute x6 -> x0, starting transfers between devices: 28.8 us -> none  [the longest x3 20.9 us: padded(): after = lax.ppermute(leading, axis, down)]
    all_to_all x2 -> x0, starting transfers between devices: 25.6 us -> none  [the longest x1 21.1 us: summed_on_arrival(): pieces = lax.all_to_all(cut_along(value, dim, size), axis, 0, 0, tiled=True)]
    all_to_all x2 -> x0, waiting for transfers between devices: 25.1 us -> none  [the longest x1 14 us: copy_for_each(): lax.all_to_all(jnp.broadcast_to(value[None], (size, *value.shape)), axis,...]
    add x12 -> x0, other arithmetic: 7.27 us -> none  [the longest x8 4.91 us: taylor_deep(): image = -0.5 * lap + local_pot[None, None] * term[:, :, 2:width + 2]]
    another operation x48 -> x0, other arithmetic: 3.3 us -> none  [next_term(): jnp.stack([time_step * image[1] / order, -time_step * image[0] / order])]
    slice x14 -> x0, local copies, waits for them, and re-layouts: 3.15 us -> none  [the longest x4 1.76 us: second_local(): far = jnp.roll(field, 2, axis) + jnp.roll(field, -2, axis)]
  transfers between devices with their start and end apart: 8 -> 0, of which waited for: 4 -> 0; matrix products, arithmetic and copies ran while one was open for 3% -> 0% of each run, Pallas kernels for 0% -> 0%
where the time goes in v1:
time: 61.8 us; the launch traced here: 61.6 us
  Pallas kernels  58.1 us (94%)
  local copies, waits for them, and re-layouts  2.23 us (4%)
  between operations  1.29 us (2%)
    pallas_call x1, Pallas kernels, shards(): pl.pallas_call(kernel, out_shape=(jax.ShapeDtypeStruct(brick, f32), jax.S...  58.1 us
    unnamed x4, local copies, waits for them, and re-layouts  2.23 us

profile of v1, /device:TPU:1, one launch (start us, length us, event | category | flops | bytes accessed | tf_op | source)
XLA Modules:
  0.0 61.6 jit_solution(14479254509180092660)
XLA Ops:
  1.3 58.1 %shard_map.59 = (f32[2,8,16,128]{3,2,1,0:T(8,128)}, f32[8,16,128]{2,1,0:T(8,128)}) custom-call(f32[1]{0:T(128)S(6)} %copy.9.occ_ref, f32[2,8,16,128]{3,2,1,0:T(8,128)} %bitcast.4, f32[8,16,128]{2,1,0:T(8,128)} %core_hbm.1, f32[8,16,128]{2,1,0:T(8,128)} %ext_hbm.1), custom_call_target="tpu_custom_call" | custom-call | tf_op jit(solution)/shard_map/pallas_call | solution.py:285
  59.4 0.0 copy-start
  59.4 1.6 %copy.10 = f32[2,1,8,16,128]{4,3,2,1,0:T(8,128)} copy(f32[2,1,8,16,128]{4,3,2,1,0:T(8,128)} %bitcast.5) | data formatting | bytes 262144
  61.0 0.0 copy-done
  61.0 0.6 %copy.11 = f32[8,16,128]{2,1,0:T(8,128)} copy(f32[8,16,128]{2,1,0:T(8,128)S(1)} %copy-done) | data formatting | bytes 131072
Async XLA Ops:
  59.4 1.6 %copy-start = (f32[8,16,128]{2,1,0:T(8,128)S(1)}, f32[8,16,128]{2,1,0:T(8,128)}, u32[]{:S(2)}) copy-start(f32[8,16,128]{2,1,0:T(8,128)} %get-tuple-element.11) | copy-start | bytes 196612
